TPU v7x, 256 devices: a whole 4x4x8 slice. The times are simulated.
256 devices in a mesh: dp: 16 (over x_lo, z), tensor: 16 (over y, x_hi, core).
Axes of the slice: x: 4 (x_hi: 2, x_lo: 2; x = x_hi * 2 + x_lo), y: 4, z: 8, core: 2. Of those that a mesh axis runs over, the one named last changes fastest.
Arguments:
- query_rows: bfloat16 [32768, 8192], P('dp', 'tensor'), may hold values from -16 to 16
- key_rows: bfloat16 [32768, 1024], P('dp'), may hold values from -10 to 10
- value_rows: bfloat16 [32768, 1024], P('dp'), may hold values from -600 to 600
- segment_ids: int32 [32768], P('dp'), may hold values from 0 to 127, never falling along the last dimension, each value on 1 to 512 neighbouring positions
- norm_gain: float32 [8192], replicated, may hold values from 0.1 to 1.9
- draft_weight: bfloat16 [8192, 512], P('tensor', 'dp'), may hold values from -0.0625 to 0.0625
- targets: bfloat16 [32768, 512], P(('dp', 'tensor')), may hold values from -6 to 6
Outputs:
- grad_weight: float32 [8192, 512], P('tensor', 'dp')
Inputs may be any that keep to these rules, and one draw needn't show every extreme that they name: `segment_ids`: document ids never fall along the tokens; a document has at most 512 tokens, and one has exactly 512.
All inputs are finite; a program needn't handle non-finite values.
Results may differ from a plain program's by a relative error of at most 0.0015.
Values may be sent and summed in bfloat16 or wider, within the bound.
No kernel may reach another device: no remote copies, remote signals or barrier semaphores. Data moves between devices by JAX's collectives and lax.ppermute only.
A program may use at most 128 MiB of HBM per device.

v0:
```python
import jax
import jax.numpy as jnp
from jax import lax
from jax.sharding import PartitionSpec as P

HEADS = 64
KV_HEADS = 8
HEAD_DIM = 128


def attend_local(query_rows, key_rows, value_rows, segment_ids):
    length = query_rows.shape[0]
    local_heads = query_rows.shape[1] // HEAD_DIM
    group = HEADS // KV_HEADS
    head_count = max(1, local_heads // group)
    repeats = local_heads // head_count
    first = lax.axis_index("tensor") * local_heads // group
    keys_local = lax.dynamic_slice_in_dim(
        key_rows, first * HEAD_DIM, head_count * HEAD_DIM, 1
    ).reshape(length, head_count, HEAD_DIM)
    values_local = lax.dynamic_slice_in_dim(
        value_rows, first * HEAD_DIM, head_count * HEAD_DIM, 1
    ).reshape(length, head_count, HEAD_DIM)
    grouped = query_rows.reshape(length, head_count, repeats, HEAD_DIM)
    width = min(length, 512)
    scale = HEAD_DIM ** (-0.5)
    places = jnp.arange(length, dtype=jnp.int32)

    def one_block(number):
        offset = number * width
        query_block = lax.dynamic_slice_in_dim(grouped, offset, width, 0)
        block_segments = lax.dynamic_slice_in_dim(segment_ids, offset, width, 0)
        block_places = offset + jnp.arange(width, dtype=jnp.int32)
        allowed = (block_segments[:, None] == segment_ids[None, :]) & (
            block_places[:, None] >= places[None, :]
        )
        scores = (
            jnp.einsum(
                "qgrd,kgd->grqk", query_block, keys_local, preferred_element_type=jnp.float32
            )
            * scale
        )
        scores = jnp.where(allowed[None, None], scores, -1e30)
        shifted = jnp.exp(scores - jnp.max(scores, axis=-1, keepdims=True))
        probs = (shifted / jnp.sum(shifted, axis=-1, keepdims=True)).astype(jnp.bfloat16)
        mixed = jnp.einsum(
            "grqk,kgd->qgrd", probs, values_local, preferred_element_type=jnp.float32
        )
        return mixed.astype(jnp.bfloat16).reshape(width, local_heads * HEAD_DIM)

    outputs = lax.map(one_block, jnp.arange(length // width, dtype=jnp.int32))
    return outputs.reshape(length, local_heads * HEAD_DIM)


def loss_derivative(predicted, targets, total_tokens):
    residual = predicted - targets.astype(jnp.float32)
    return (jnp.clip(residual, -1.0, 1.0) / jnp.sqrt(jnp.float32(total_tokens))).astype(
        jnp.bfloat16
    )


def on_device(query_rows, key_rows, value_rows, segment_ids, norm_gain, draft_weight, targets):
    attended = attend_local(query_rows, key_rows, value_rows, segment_ids)
    length = query_rows.shape[0]
    total_tokens = length * lax.axis_size("dp")
    weight_slab = lax.all_gather(draft_weight, "dp", axis=1, tiled=True)
    regrouped = lax.all_to_all(attended, "tensor", split_axis=0, concat_axis=1, tiled=True)
    features = regrouped.astype(jnp.float32)
    mean_square = jnp.mean(features * features, axis=-1, keepdims=True)
    normed = (features * lax.rsqrt(mean_square + 1e-06) * norm_gain[None, :]).astype(jnp.bfloat16)
    picked = normed
    predicted = jnp.dot(
        picked,
        lax.all_gather(weight_slab, "tensor", axis=0, tiled=True),
        preferred_element_type=jnp.float32,
    )
    grad_pred = loss_derivative(predicted, targets, total_tokens)
    picked = normed
    grad_slab = lax.psum_scatter(
        lax.dot_general(
            picked, grad_pred, (((0,), (0,)), ((), ())), preferred_element_type=jnp.float32
        ),
        "tensor",
        scatter_dimension=0,
        tiled=True,
    )
    return lax.psum_scatter(grad_slab, "dp", scatter_dimension=1, tiled=True)


def solution(mesh):
    placed = (
        P("dp", "tensor"),
        P("dp", None),
        P("dp", None),
        P("dp"),
        P(),
        P("tensor", "dp"),
        P(("dp", "tensor"), None),
    )
    return jax.shard_map(
        on_device, mesh=mesh, in_specs=placed, out_specs=P("tensor", "dp"), check_vma=False
    )
```

profile of v0, /device:TPU:8, one launch (start us, length us, event | category | flops | bytes accessed | tf_op | source)
XLA Modules:
  0.0 414.3 jit_solution(10289684197386694751)
XLA Ops:
  6.5 41.8 %all_gather.6 = bf16[512,512]{0,1:T(8,128)(2,1)} all-gather(bf16[512,32]{0,1:T(8,128)(2,1)} %param.14), channel_id=1, replica_groups=mesh['dp'=16,'tensor'=16] {'dp'}, dimensions={1}, use_global_device_ids=true | all-gather | bytes 557056 | tf_op jit(solution)/shard_map/all_gather | solution.py:66
  48.5 1.1 constant_dynamic-slice_fusion
  49.5 0.2 copy.17
  49.8 1.1 dynamic-slice_bitcast_fusion
  50.9 2.5 copy.16
  53.4 73.3 %while.11 = (s32[]{:T(128)}, bf16[4,512,512]{2,1,0:T(8,128)(2,1)}, s32[4]{0:T(128)S(1)}, s32[2048]{0:T(1024)S(1)}, bf16[2048,1,4,128]{0,3,2,1:T(8,128)(2,1)}, /*...) while((s32[]{:T(128)}, bf16[4,512,512]{2,1,0:T(8,128)(2,1)}, ...), condition=%wide.region_3.4_spmd.clone, body=%wide.region_0.3_spmd.clone.sunk | while | flops 2201219584 | bytes 58780336 | solution.py:51
  53.4 0.6 dynamic_slice.33
  54.7 0.1 dynamic_slice.34
  54.8 1.2 fusion.37
  56.0 4.9 %fusion.38 = (f32[4,512]{1,0:T(4,128)S(1)}, f32[512,4,2048]{2,0,1:T(8,128)S(1)}) fusion(pred[512,2048]{1,0:T(8,128)(4,1)S(1)} %fusion.37, bf16[2048,1,128]{2,0,1:T(8,128)(2,1)S(1)} %get-tuple-element.168, bf16[2048,1,4,128]{0,3,2,1:T(8,128)(2,1)} %get-tuple-element.167, s32[]{:T(128)S(6)} %select_n.40), kind=kOutput, calls=%fused_computation.5.clone.1 | convolution fusion | flops 1086322688 | bytes 18882564 | tf_op jit(solution)/shard_map/while/body/eval_jaxpr/qgrd,kgd->grqk/dot_general | solution.py:38
  60.9 4.5 %fusion.39 = f32[4,512]{1,0:T(4,128)S(1)} fusion(f32[512,4,2048]{2,0,1:T(8,128)S(1)} %get-tuple-element.139, f32[4,512]{1,0:T(4,128)S(1)} %get-tuple-element.140, pred[512,2048]{1,0:T(8,128)(4,1)S(1)} %fusion.37), kind=kLoop, calls=%fused_computation.4.clone.1 | loop fusion | flops 16775168 | bytes 17842176 | tf_op jit(solution)/shard_map/while/body/eval_jaxpr/reduce_sum | solution.py:45
  65.4 5.3 %fusion.40 = bf16[4,512,128]{1,2,0:T(8,128)(2,1)S(1)} fusion(f32[4,512]{1,0:T(4,128)S(1)} %fusion.39, f32[4,512]{1,0:T(4,128)S(1)} %get-tuple-element.140, f32[512,4,2048]{2,0,1:T(8,128)S(1)} %get-tuple-element.139, pred[512,2048]{1,0:T(8,128)(4,1)S(1)} %fusion.37, bf16[2048,1,128]{0,2,1:T(8,128)(2,1)S(1)} %get-tuple-element.169), kind=kOutput, calls=%fused_computation.10.clone.1 | convolution fusion | flops 1094975488 | bytes 18890752 | tf_op jit(solution)/shard_map/while/body/eval_jaxpr/grqk,kgd->qgrd/dot_general | solution.py:46
  70.7 0.2 copy.28
  70.9 0.9 constant_dynamic-update-slice_fusion.2
  71.7 0.6 dynamic_slice.33
  73.1 0.1 dynamic_slice.34
  73.2 1.2 fusion.37
  74.4 4.9 %fusion.38 = (f32[4,512]{1,0:T(4,128)S(1)}, f32[512,4,2048]{2,0,1:T(8,128)S(1)}) fusion(pred[512,2048]{1,0:T(8,128)(4,1)S(1)} %fusion.37, bf16[2048,1,128]{2,0,1:T(8,128)(2,1)S(1)} %get-tuple-element.168, bf16[2048,1,4,128]{0,3,2,1:T(8,128)(2,1)} %get-tuple-element.167, s32[]{:T(128)S(6)} %select_n.40), kind=kOutput, calls=%fused_computation.5.clone.1 | convolution fusion | flops 1086322688 | bytes 18882564 | tf_op jit(solution)/shard_map/while/body/eval_jaxpr/qgrd,kgd->grqk/dot_general | solution.py:38
  79.2 4.5 %fusion.39 = f32[4,512]{1,0:T(4,128)S(1)} fusion(f32[512,4,2048]{2,0,1:T(8,128)S(1)} %get-tuple-element.139, f32[4,512]{1,0:T(4,128)S(1)} %get-tuple-element.140, pred[512,2048]{1,0:T(8,128)(4,1)S(1)} %fusion.37), kind=kLoop, calls=%fused_computation.4.clone.1 | loop fusion | flops 16775168 | bytes 17842176 | tf_op jit(solution)/shard_map/while/body/eval_jaxpr/reduce_sum | solution.py:45
  83.7 5.3 %fusion.40 = bf16[4,512,128]{1,2,0:T(8,128)(2,1)S(1)} fusion(f32[4,512]{1,0:T(4,128)S(1)} %fusion.39, f32[4,512]{1,0:T(4,128)S(1)} %get-tuple-element.140, f32[512,4,2048]{2,0,1:T(8,128)S(1)} %get-tuple-element.139, pred[512,2048]{1,0:T(8,128)(4,1)S(1)} %fusion.37, bf16[2048,1,128]{0,2,1:T(8,128)(2,1)S(1)} %get-tuple-element.169), kind=kOutput, calls=%fused_computation.10.clone.1 | convolution fusion | flops 1094975488 | bytes 18890752 | tf_op jit(solution)/shard_map/while/body/eval_jaxpr/grqk,kgd->qgrd/dot_general | solution.py:46
  89.0 0.2 copy.28
  89.2 0.8 constant_dynamic-update-slice_fusion.2
  90.1 0.6 dynamic_slice.33
  91.4 0.1 dynamic_slice.34
  91.5 1.2 fusion.37
  92.7 4.9 %fusion.38 = (f32[4,512]{1,0:T(4,128)S(1)}, f32[512,4,2048]{2,0,1:T(8,128)S(1)}) fusion(pred[512,2048]{1,0:T(8,128)(4,1)S(1)} %fusion.37, bf16[2048,1,128]{2,0,1:T(8,128)(2,1)S(1)} %get-tuple-element.168, bf16[2048,1,4,128]{0,3,2,1:T(8,128)(2,1)} %get-tuple-element.167, s32[]{:T(128)S(6)} %select_n.40), kind=kOutput, calls=%fused_computation.5.clone.1 | convolution fusion | flops 1086322688 | bytes 18882564 | tf_op jit(solution)/shard_map/while/body/eval_jaxpr/qgrd,kgd->grqk/dot_general | solution.py:38
  97.6 4.5 %fusion.39 = f32[4,512]{1,0:T(4,128)S(1)} fusion(f32[512,4,2048]{2,0,1:T(8,128)S(1)} %get-tuple-element.139, f32[4,512]{1,0:T(4,128)S(1)} %get-tuple-element.140, pred[512,2048]{1,0:T(8,128)(4,1)S(1)} %fusion.37), kind=kLoop, calls=%fused_computation.4.clone.1 | loop fusion | flops 16775168 | bytes 17842176 | tf_op jit(solution)/shard_map/while/body/eval_jaxpr/reduce_sum | solution.py:45
  102.1 5.3 %fusion.40 = bf16[4,512,128]{1,2,0:T(8,128)(2,1)S(1)} fusion(f32[4,512]{1,0:T(4,128)S(1)} %fusion.39, f32[4,512]{1,0:T(4,128)S(1)} %get-tuple-element.140, f32[512,4,2048]{2,0,1:T(8,128)S(1)} %get-tuple-element.139, pred[512,2048]{1,0:T(8,128)(4,1)S(1)} %fusion.37, bf16[2048,1,128]{0,2,1:T(8,128)(2,1)S(1)} %get-tuple-element.169), kind=kOutput, calls=%fused_computation.10.clone.1 | convolution fusion | flops 1094975488 | bytes 18890752 | tf_op jit(solution)/shard_map/while/body/eval_jaxpr/grqk,kgd->qgrd/dot_general | solution.py:46
  107.3 0.2 copy.28
  107.6 0.8 constant_dynamic-update-slice_fusion.2
  108.4 0.6 dynamic_slice.33
  109.7 0.1 dynamic_slice.34
  109.8 1.2 fusion.37
  111.0 4.9 %fusion.38 = (f32[4,512]{1,0:T(4,128)S(1)}, f32[512,4,2048]{2,0,1:T(8,128)S(1)}) fusion(pred[512,2048]{1,0:T(8,128)(4,1)S(1)} %fusion.37, bf16[2048,1,128]{2,0,1:T(8,128)(2,1)S(1)} %get-tuple-element.168, bf16[2048,1,4,128]{0,3,2,1:T(8,128)(2,1)} %get-tuple-element.167, s32[]{:T(128)S(6)} %select_n.40), kind=kOutput, calls=%fused_computation.5.clone.1 | convolution fusion | flops 1086322688 | bytes 18882564 | tf_op jit(solution)/shard_map/while/body/eval_jaxpr/qgrd,kgd->grqk/dot_general | solution.py:38
  115.9 4.5 %fusion.39 = f32[4,512]{1,0:T(4,128)S(1)} fusion(f32[512,4,2048]{2,0,1:T(8,128)S(1)} %get-tuple-element.139, f32[4,512]{1,0:T(4,128)S(1)} %get-tuple-element.140, pred[512,2048]{1,0:T(8,128)(4,1)S(1)} %fusion.37), kind=kLoop, calls=%fused_computation.4.clone.1 | loop fusion | flops 16775168 | bytes 17842176 | tf_op jit(solution)/shard_map/while/body/eval_jaxpr/reduce_sum | solution.py:45
  120.4 5.3 %fusion.40 = bf16[4,512,128]{1,2,0:T(8,128)(2,1)S(1)} fusion(f32[4,512]{1,0:T(4,128)S(1)} %fusion.39, f32[4,512]{1,0:T(4,128)S(1)} %get-tuple-element.140, f32[512,4,2048]{2,0,1:T(8,128)S(1)} %get-tuple-element.139, pred[512,2048]{1,0:T(8,128)(4,1)S(1)} %fusion.37, bf16[2048,1,128]{0,2,1:T(8,128)(2,1)S(1)} %get-tuple-element.169), kind=kOutput, calls=%fused_computation.10.clone.1 | convolution fusion | flops 1094975488 | bytes 18890752 | tf_op jit(solution)/shard_map/while/body/eval_jaxpr/grqk,kgd->qgrd/dot_general | solution.py:46
  125.7 0.2 copy.28
  125.9 0.9 constant_dynamic-update-slice_fusion.2
  126.7 33.7 %all_to_all.13 = bf16[16,128,512]{2,1,0:T(8,128)(2,1)S(1)} all-to-all(bf16[16,128,512]{2,1,0:T(8,128)(2,1)} %bitcast.86), channel_id=1, replica_groups=mesh['dp'=16,'tensor'=16] {'tensor'}, dimensions={0} | all-to-all | bytes 4194304 | tf_op jit(solution)/shard_map/all_to_all | solution.py:67
  160.5 2.5 convert_bitcast_fusion
  163.0 5.3 %copy.20 = f32[128,16,512]{0,2,1:T(8,128)} copy(f32[128,16,512]{2,0,1:T(8,128)} %convert_bitcast_fusion) | data formatting | bytes 8388608 | tf_op jit(solution)/shard_map/convert_element_type | solution.py:68
  168.4 0.5 fusion.18
  168.9 2.9 fusion.20
  171.8 6.3 %fusion.23 = bf16[128,512]{1,0:T(8,128)(2,1)S(1)} fusion(bf16[128,8192]{0,1:T(8,128)(2,1)S(1)} %fusion.20, bf16[8192,512]{0,1:T(8,128)(2,1)} %all-gather.2.cloned.1.call-done, bf16[128,512]{1,0:T(8,128)(2,1)S(1)} %copy-done.2), kind=kOutput, calls=%fused_computation.30 | convolution fusion | flops 1074069504 | bytes 10747904 | tf_op jit(solution)/shard_map/dot_general | solution.py:72
  178.1 8.0 %fusion.24 = f32[8192,512]{1,0:T(8,128)} fusion(bf16[128,8192]{0,1:T(8,128)(2,1)S(1)} %fusion.20, bf16[128,512]{1,0:T(8,128)(2,1)S(1)} %fusion.23), kind=kOutput, calls=%fused_computation.34 | convolution fusion | flops 1073741824 | bytes 19005440 | tf_op jit(solution)/shard_map/dot_general | solution.py:80
  186.2 147.4 %reduce-scatter.5.cloned.1.call-done = f32[512,512]{1,0:T(8,128)} async-done(((f32[8192,512]{1,0:T(8,128)}), f32[512,512]{1,0:T(8,128)}) %reduce-scatter.5.cloned.1.call-update) | async-done | bytes 1048592 | tf_op jit(solution)/shard_map/reduce_scatter | solution.py:79
  333.6 2.5 copy.22
  336.1 71.6 %reduce-scatter.7.cloned.1.call-done = f32[32,512]{1,0:T(8,128)} async-done(((f32[512,512]{1,0:T(8,128)}), f32[32,512]{1,0:T(8,128)}) %reduce-scatter.7.cloned.1.call-update) | async-done | bytes 65552
  (22 shorter events, 0.2 us)
Async XLA Ops:
  6.5 44.3 %copy-start = (bf16[2048,512]{1,0:T(8,128)(2,1)S(1)}, bf16[2048,512]{1,0:T(8,128)(2,1)}, u32[]{:S(2)}) copy-start(bf16[2048,512]{1,0:T(8,128)(2,1)} %param.9) | copy-start | bytes 6291460
  6.5 46.9 %copy-start.1 = (s32[2048]{0:T(1024)S(1)}, s32[2048]{0:T(1024)}, u32[]{:S(2)}) copy-start(s32[2048]{0:T(1024)} %param.12) | copy-start | bytes 24580
  6.5 165.2 %all-gather.2.cloned.1.call-start = ((), (), s32[]{:S(2)}) async-start(), calls=%async_computation.3 | async-start | bytes 8912896 | tf_op jit(solution)/shard_map/all_gather | solution.py:74
  48.4 285.2 %reduce-scatter.5.cloned.1.call-start = ((), (), s32[]{:S(2)}) async-start(), calls=%async_computation.4 | async-start | bytes 17825792 | tf_op jit(solution)/shard_map/reduce_scatter | solution.py:79
  163.0 5.9 %copy-start.3 = (f32[8192]{0:T(1024)S(1)}, f32[8192]{0:T(1024)}, u32[]{:S(2)}) copy-start(f32[8192]{0:T(1024)} %param.13) | copy-start | bytes 98308
  168.4 3.4 copy-start.2
  186.1 221.6 %reduce-scatter.7.cloned.1.call-start = ((), (), s32[]{:S(2)}) async-start(), calls=%async_computation.5 | async-start | bytes 1114112
Sparse Core Ops, SparseCore 0:
  48.5 75.7 all-gather.1
  186.2 147.2 reduce-scatter.4
  336.3 71.4 reduce-scatter.6
where the time goes:
time: 415 us; the launch traced here: 414 us
  waiting for transfers between devices  219 us (53%)
  blocking collectives  75.5 us (18%)
  matrix products  55 us (13%)
  other arithmetic  28.6 us (7%)
  local copies, waits for them, and re-layouts  20 us (5%)
  between operations  13.2 us (3%)
    reduce_scatter x1, waiting for transfers between devices, on_device(): lax.psum_scatter(lax.dot_general(picked, grad_pred, (((0,), (0,)), ((), (...  147 us
    unnamed x4, waiting for transfers between devices  71.7 us
    all_gather x1, blocking collectives, on_device(): weight_slab = lax.all_gather(draft_weight, 'dp', axis=1, tiled=True)  41.8 us
    all_to_all x1, blocking collectives, on_device(): lax.all_to_all(attended, 'tensor', split_axis=0, concat_axis=1, tiled=True)  33.7 us
    dot_general x4, matrix products, one_block(): jnp.einsum('grqk,kgd->qgrd', probs, values_local, preferred_element_type=...  21.1 us
    dot_general x4, matrix products, one_block(): jnp.einsum('qgrd,kgd->grqk', query_block, keys_local, preferred_element_t...  19.5 us
    reduce_sum x4, other arithmetic, one_block(): jnp.sum(shifted, axis=-1, keepdims=True)  17.9 us
  transfers between devices with their start and end apart: 3, of which 2 were waited for; matrix products, arithmetic and copies ran while one was open for 21% of the time, Pallas kernels for 0%

commit v1 on v0

--- a/solution.py
+++ b/solution.py
@@ -63,7 +63,9 @@
     attended = attend_local(query_rows, key_rows, value_rows, segment_ids)
     length = query_rows.shape[0]
     total_tokens = length * lax.axis_size("dp")
-    weight_slab = lax.all_gather(draft_weight, "dp", axis=1, tiled=True)
+    weight_slab = jnp.concatenate(
+        lax.all_to_all(jnp.stack([draft_weight] * lax.axis_size("dp")), "dp", 0, 0), axis=1
+    )
     regrouped = lax.all_to_all(attended, "tensor", split_axis=0, concat_axis=1, tiled=True)
     features = regrouped.astype(jnp.float32)
     mean_square = jnp.mean(features * features, axis=-1, keepdims=True)

time: 415 us -> 398 us (0.959)
  blocking collectives: 75.5 us -> 33.7 us
  waiting for transfers between devices: 219 us -> 231 us
  starting transfers between devices: 0.08 us -> 9.62 us
    all_gather x1 -> x0, blocking collectives: 41.8 us -> none  [on_device(): weight_slab = lax.all_gather(draft_weight, 'dp', axis=1, tiled=True)]
    all_to_all x0 -> x1, waiting for transfers between devices: none -> 9.89 us  [on_device(): lax.all_to_all(jnp.stack([draft_weight] * lax.axis_size('dp')), 'dp', 0, 0)]
    all_to_all x0 -> x1, starting transfers between devices: none -> 9.5 us  [on_device(): lax.all_to_all(jnp.stack([draft_weight] * lax.axis_size('dp')), 'dp', 0, 0)]
  transfers between devices with their start and end apart: 3 -> 4, of which waited for: 2 -> 3; matrix products, arithmetic and copies ran while one was open for 21% -> 22% of each run, Pallas kernels for 0% -> 0%
where the time goes in v1:
time: 398 us; the launch traced here: 397 us
  waiting for transfers between devices  231 us (58%)
  matrix products  55 us (14%)
  blocking collectives  33.7 us (8%)
  other arithmetic  28.5 us (7%)
  local copies, waits for them, and re-layouts  23 us (6%)
  between operations  13.2 us (3%)
  starting transfers between devices  9.62 us (2%)
    reduce_scatter x1, waiting for transfers between devices, on_device(): lax.psum_scatter(lax.dot_general(picked, grad_pred, (((0,), (0,)), ((), (...  150 us
    unnamed x4, waiting for transfers between devices  71.8 us
    all_to_all x1, blocking collectives, on_device(): lax.all_to_all(attended, 'tensor', split_axis=0, concat_axis=1, tiled=True)  33.7 us
    dot_general x4, matrix products, one_block(): jnp.einsum('grqk,kgd->qgrd', probs, values_local, preferred_element_type=...  21.1 us
    dot_general x4, matrix products, one_block(): jnp.einsum('qgrd,kgd->grqk', query_block, keys_local, preferred_element_t...  19.5 us
    reduce_sum x4, other arithmetic, one_block(): jnp.sum(shifted, axis=-1, keepdims=True)  17.9 us
    all_to_all x1, waiting for transfers between devices, on_device(): lax.all_to_all(jnp.stack([draft_weight] * lax.axis_size('dp')), 'dp', 0, 0)  9.89 us
    all_to_all x1, starting transfers between devices, on_device(): lax.all_to_all(jnp.stack([draft_weight] * lax.axis_size('dp')), 'dp', 0, 0)  9.5 us
  transfers between devices with their start and end apart: 4, of which 3 were waited for; matrix products, arithmetic and copies ran while one was open for 22% of the time, Pallas kernels for 0%

profile of v1, /device:TPU:8, one launch (start us, length us, event | category | flops | bytes accessed | tf_op | source)
XLA Modules:
  0.0 397.1 jit_solution(16283340770302144688)
XLA Ops:
  6.5 1.8 stack.2
  8.3 9.5 %all-to-all-start.1 = ((bf16[16,512,32]{1,2,0:T(8,128)(2,1)}), bf16[16,512,32]{1,2,0:T(8,128)(2,1)S(1)}, u32[]{:S(2)}, u32[]{:S(2)}) async-start(bf16[16,512,32]{1,2,0:T(8,128)(2,1)} %stack.2), calls=%async_computation.1 | async-start | bytes 1048576 | tf_op jit(solution)/shard_map/all_to_all | solution.py:67
  17.9 1.1 constant_dynamic-slice_fusion
  19.0 1.0 copy.18
  20.0 2.5 copy.17
  22.5 1.1 dynamic-slice_bitcast_fusion
  23.6 9.9 %all-to-all-done.1 = bf16[16,512,32]{1,2,0:T(8,128)(2,1)S(1)} async-done(((bf16[16,512,32]{1,2,0:T(8,128)(2,1)}), bf16[16,512,32]{1,2,0:T(8,128)(2,1)S(1)}, u32[]{:S(2)}, u32[]{:S(2)}) %all-to-all-start.1) | async-done | bytes 524320 | tf_op jit(solution)/shard_map/all_to_all | solution.py:67
  33.5 0.8 copy-done.1
  34.4 72.9 %while.11 = (s32[]{:T(128)}, bf16[4,512,512]{2,1,0:T(8,128)(2,1)}, s32[4]{0:T(128)S(1)}, s32[2048]{0:T(1024)S(1)}, bf16[2048,1,4,128]{0,3,2,1:T(8,128)(2,1)}, /*...) while((s32[]{:T(128)}, bf16[4,512,512]{2,1,0:T(8,128)(2,1)}, ...), condition=%wide.region_3.4_spmd.clone, body=%wide.region_0.3_spmd.clone.sunk | while | flops 2201219584 | bytes 58780336 | solution.py:51
  34.4 0.6 dynamic_slice.33
  35.6 0.1 dynamic_slice.34
  35.7 1.2 fusion.37
  36.9 4.9 %fusion.38 = (f32[4,512]{1,0:T(4,128)S(1)}, f32[512,4,2048]{2,0,1:T(8,128)S(1)}) fusion(pred[512,2048]{1,0:T(8,128)(4,1)S(1)} %fusion.37, bf16[2048,1,128]{2,0,1:T(8,128)(2,1)S(1)} %get-tuple-element.168, bf16[2048,1,4,128]{0,3,2,1:T(8,128)(2,1)} %get-tuple-element.167, s32[]{:T(128)S(6)} %select_n.40), kind=kOutput, calls=%fused_computation.5.clone.1 | convolution fusion | flops 1086322688 | bytes 18882564 | tf_op jit(solution)/shard_map/while/body/eval_jaxpr/qgrd,kgd->grqk/dot_general | solution.py:38
  41.8 4.5 %fusion.39 = f32[4,512]{1,0:T(4,128)S(1)} fusion(f32[512,4,2048]{2,0,1:T(8,128)S(1)} %get-tuple-element.139, f32[4,512]{1,0:T(4,128)S(1)} %get-tuple-element.140, pred[512,2048]{1,0:T(8,128)(4,1)S(1)} %fusion.37), kind=kLoop, calls=%fused_computation.4.clone.1 | loop fusion | flops 16775168 | bytes 17842176 | tf_op jit(solution)/shard_map/while/body/eval_jaxpr/reduce_sum | solution.py:45
  46.3 5.3 %fusion.40 = bf16[4,512,128]{1,2,0:T(8,128)(2,1)S(1)} fusion(f32[4,512]{1,0:T(4,128)S(1)} %fusion.39, f32[4,512]{1,0:T(4,128)S(1)} %get-tuple-element.140, f32[512,4,2048]{2,0,1:T(8,128)S(1)} %get-tuple-element.139, pred[512,2048]{1,0:T(8,128)(4,1)S(1)} %fusion.37, bf16[2048,1,128]{0,2,1:T(8,128)(2,1)S(1)} %get-tuple-element.169), kind=kOutput, calls=%fused_computation.10.clone.1 | convolution fusion | flops 1094975488 | bytes 18890752 | tf_op jit(solution)/shard_map/while/body/eval_jaxpr/grqk,kgd->qgrd/dot_general | solution.py:46
  51.5 0.2 copy.29
  51.8 0.8 constant_dynamic-update-slice_fusion.2
  52.6 0.6 dynamic_slice.33
  53.9 1.2 fusion.37
  55.1 4.9 %fusion.38 = (f32[4,512]{1,0:T(4,128)S(1)}, f32[512,4,2048]{2,0,1:T(8,128)S(1)}) fusion(pred[512,2048]{1,0:T(8,128)(4,1)S(1)} %fusion.37, bf16[2048,1,128]{2,0,1:T(8,128)(2,1)S(1)} %get-tuple-element.168, bf16[2048,1,4,128]{0,3,2,1:T(8,128)(2,1)} %get-tuple-element.167, s32[]{:T(128)S(6)} %select_n.40), kind=kOutput, calls=%fused_computation.5.clone.1 | convolution fusion | flops 1086322688 | bytes 18882564 | tf_op jit(solution)/shard_map/while/body/eval_jaxpr/qgrd,kgd->grqk/dot_general | solution.py:38
  60.0 4.5 %fusion.39 = f32[4,512]{1,0:T(4,128)S(1)} fusion(f32[512,4,2048]{2,0,1:T(8,128)S(1)} %get-tuple-element.139, f32[4,512]{1,0:T(4,128)S(1)} %get-tuple-element.140, pred[512,2048]{1,0:T(8,128)(4,1)S(1)} %fusion.37), kind=kLoop, calls=%fused_computation.4.clone.1 | loop fusion | flops 16775168 | bytes 17842176 | tf_op jit(solution)/shard_map/while/body/eval_jaxpr/reduce_sum | solution.py:45
  64.5 5.3 %fusion.40 = bf16[4,512,128]{1,2,0:T(8,128)(2,1)S(1)} fusion(f32[4,512]{1,0:T(4,128)S(1)} %fusion.39, f32[4,512]{1,0:T(4,128)S(1)} %get-tuple-element.140, f32[512,4,2048]{2,0,1:T(8,128)S(1)} %get-tuple-element.139, pred[512,2048]{1,0:T(8,128)(4,1)S(1)} %fusion.37, bf16[2048,1,128]{0,2,1:T(8,128)(2,1)S(1)} %get-tuple-element.169), kind=kOutput, calls=%fused_computation.10.clone.1 | convolution fusion | flops 1094975488 | bytes 18890752 | tf_op jit(solution)/shard_map/while/body/eval_jaxpr/grqk,kgd->qgrd/dot_general | solution.py:46
  69.8 0.2 copy.29
  70.0 0.8 constant_dynamic-update-slice_fusion.2
  70.8 0.6 dynamic_slice.33
  72.1 1.2 fusion.37
  73.3 4.9 %fusion.38 = (f32[4,512]{1,0:T(4,128)S(1)}, f32[512,4,2048]{2,0,1:T(8,128)S(1)}) fusion(pred[512,2048]{1,0:T(8,128)(4,1)S(1)} %fusion.37, bf16[2048,1,128]{2,0,1:T(8,128)(2,1)S(1)} %get-tuple-element.168, bf16[2048,1,4,128]{0,3,2,1:T(8,128)(2,1)} %get-tuple-element.167, s32[]{:T(128)S(6)} %select_n.40), kind=kOutput, calls=%fused_computation.5.clone.1 | convolution fusion | flops 1086322688 | bytes 18882564 | tf_op jit(solution)/shard_map/while/body/eval_jaxpr/qgrd,kgd->grqk/dot_general | solution.py:38
  78.2 4.5 %fusion.39 = f32[4,512]{1,0:T(4,128)S(1)} fusion(f32[512,4,2048]{2,0,1:T(8,128)S(1)} %get-tuple-element.139, f32[4,512]{1,0:T(4,128)S(1)} %get-tuple-element.140, pred[512,2048]{1,0:T(8,128)(4,1)S(1)} %fusion.37), kind=kLoop, calls=%fused_computation.4.clone.1 | loop fusion | flops 16775168 | bytes 17842176 | tf_op jit(solution)/shard_map/while/body/eval_jaxpr/reduce_sum | solution.py:45
  82.7 5.3 %fusion.40 = bf16[4,512,128]{1,2,0:T(8,128)(2,1)S(1)} fusion(f32[4,512]{1,0:T(4,128)S(1)} %fusion.39, f32[4,512]{1,0:T(4,128)S(1)} %get-tuple-element.140, f32[512,4,2048]{2,0,1:T(8,128)S(1)} %get-tuple-element.139, pred[512,2048]{1,0:T(8,128)(4,1)S(1)} %fusion.37, bf16[2048,1,128]{0,2,1:T(8,128)(2,1)S(1)} %get-tuple-element.169), kind=kOutput, calls=%fused_computation.10.clone.1 | convolution fusion | flops 1094975488 | bytes 18890752 | tf_op jit(solution)/shard_map/while/body/eval_jaxpr/grqk,kgd->qgrd/dot_general | solution.py:46
  88.0 0.2 copy.29
  88.2 0.8 constant_dynamic-update-slice_fusion.2
  89.0 0.6 dynamic_slice.33
  90.3 1.2 fusion.37
  91.5 4.9 %fusion.38 = (f32[4,512]{1,0:T(4,128)S(1)}, f32[512,4,2048]{2,0,1:T(8,128)S(1)}) fusion(pred[512,2048]{1,0:T(8,128)(4,1)S(1)} %fusion.37, bf16[2048,1,128]{2,0,1:T(8,128)(2,1)S(1)} %get-tuple-element.168, bf16[2048,1,4,128]{0,3,2,1:T(8,128)(2,1)} %get-tuple-element.167, s32[]{:T(128)S(6)} %select_n.40), kind=kOutput, calls=%fused_computation.5.clone.1 | convolution fusion | flops 1086322688 | bytes 18882564 | tf_op jit(solution)/shard_map/while/body/eval_jaxpr/qgrd,kgd->grqk/dot_general | solution.py:38
  96.4 4.5 %fusion.39 = f32[4,512]{1,0:T(4,128)S(1)} fusion(f32[512,4,2048]{2,0,1:T(8,128)S(1)} %get-tuple-element.139, f32[4,512]{1,0:T(4,128)S(1)} %get-tuple-element.140, pred[512,2048]{1,0:T(8,128)(4,1)S(1)} %fusion.37), kind=kLoop, calls=%fused_computation.4.clone.1 | loop fusion | flops 16775168 | bytes 17842176 | tf_op jit(solution)/shard_map/while/body/eval_jaxpr/reduce_sum | solution.py:45
  100.9 5.3 %fusion.40 = bf16[4,512,128]{1,2,0:T(8,128)(2,1)S(1)} fusion(f32[4,512]{1,0:T(4,128)S(1)} %fusion.39, f32[4,512]{1,0:T(4,128)S(1)} %get-tuple-element.140, f32[512,4,2048]{2,0,1:T(8,128)S(1)} %get-tuple-element.139, pred[512,2048]{1,0:T(8,128)(4,1)S(1)} %fusion.37, bf16[2048,1,128]{0,2,1:T(8,128)(2,1)S(1)} %get-tuple-element.169), kind=kOutput, calls=%fused_computation.10.clone.1 | convolution fusion | flops 1094975488 | bytes 18890752 | tf_op jit(solution)/shard_map/while/body/eval_jaxpr/grqk,kgd->qgrd/dot_general | solution.py:46
  106.2 0.2 copy.29
  106.4 0.8 constant_dynamic-update-slice_fusion.2
  107.2 33.7 %all_to_all.18 = bf16[16,128,512]{2,1,0:T(8,128)(2,1)S(1)} all-to-all(bf16[16,128,512]{2,1,0:T(8,128)(2,1)} %bitcast.89), channel_id=1, replica_groups=mesh['dp'=16,'tensor'=16] {'tensor'}, dimensions={0} | all-to-all | bytes 4194304 | tf_op jit(solution)/shard_map/all_to_all | solution.py:69
  140.9 2.5 convert_bitcast_fusion
  143.4 5.3 %copy.21 = f32[128,16,512]{0,2,1:T(8,128)} copy(f32[128,16,512]{2,0,1:T(8,128)} %convert_bitcast_fusion) | data formatting | bytes 8388608 | tf_op jit(solution)/shard_map/convert_element_type | solution.py:70
  148.8 0.5 fusion.18
  149.3 2.9 fusion.20
  152.2 6.3 %fusion.23 = bf16[128,512]{1,0:T(8,128)(2,1)S(1)} fusion(bf16[128,8192]{0,1:T(8,128)(2,1)S(1)} %fusion.20, bf16[8192,512]{0,1:T(8,128)(2,1)} %all-gather.2.cloned.1.call-done, bf16[128,512]{1,0:T(8,128)(2,1)S(1)} %copy-done.4), kind=kOutput, calls=%fused_computation.30 | convolution fusion | flops 1074069504 | bytes 10747904 | tf_op jit(solution)/shard_map/dot_general | solution.py:74
  158.5 8.0 %fusion.24 = f32[8192,512]{1,0:T(8,128)} fusion(bf16[128,8192]{0,1:T(8,128)(2,1)S(1)} %fusion.20, bf16[128,512]{1,0:T(8,128)(2,1)S(1)} %fusion.23), kind=kOutput, calls=%fused_computation.34 | convolution fusion | flops 1073741824 | bytes 19005440 | tf_op jit(solution)/shard_map/dot_general | solution.py:82
  166.6 149.7 %reduce-scatter.5.cloned.1.call-done = f32[512,512]{1,0:T(8,128)} async-done(((f32[8192,512]{1,0:T(8,128)}), f32[512,512]{1,0:T(8,128)}) %reduce-scatter.5.cloned.1.call-update) | async-done | bytes 1048592 | tf_op jit(solution)/shard_map/reduce_scatter | solution.py:81
  316.3 2.5 copy.23
  318.9 71.7 %reduce-scatter.7.cloned.1.call-done = f32[32,512]{1,0:T(8,128)} async-done(((f32[512,512]{1,0:T(8,128)}), f32[32,512]{1,0:T(8,128)}) %reduce-scatter.7.cloned.1.call-update) | async-done | bytes 65552
  (28 shorter events, 0.5 us)
Async XLA Ops:
  6.5 13.5 %copy-start = (bf16[2048,512]{1,0:T(8,128)(2,1)S(1)}, bf16[2048,512]{1,0:T(8,128)(2,1)}, u32[]{:S(2)}) copy-start(bf16[2048,512]{1,0:T(8,128)(2,1)} %param.9) | copy-start | bytes 6291460
  8.3 25.2 %all-to-all-start.1 = ((bf16[16,512,32]{1,2,0:T(8,128)(2,1)}), bf16[16,512,32]{1,2,0:T(8,128)(2,1)S(1)}, u32[]{:S(2)}, u32[]{:S(2)}) async-start(bf16[16,512,32]{1,2,0:T(8,128)(2,1)} %stack.2), calls=%async_computation.1 | async-start | bytes 1048576 | tf_op jit(solution)/shard_map/all_to_all | solution.py:67
  17.8 16.5 %copy-start.3 = (s32[2048]{0:T(1024)S(1)}, s32[2048]{0:T(1024)}, u32[]{:S(2)}) copy-start(s32[2048]{0:T(1024)} %param.12) | copy-start | bytes 24580
  17.8 134.3 %all-gather.2.cloned.1.call-start = ((), (), s32[]{:S(2)}) async-start(), calls=%async_computation.4 | async-start | bytes 8912896 | tf_op jit(solution)/shard_map/all_gather | solution.py:76
  20.0 14.3 %copy-start.2 = (bf16[2048,128]{0,1:T(8,128)(2,1)S(1)}, bf16[2048,128]{0,1:T(8,128)(2,1)}, u32[]{:S(2)}) copy-start(bf16[2048,128]{0,1:T(8,128)(2,1)} %copy.18) | copy-start | bytes 1572868
  33.5 0.8 copy-start.1
  34.3 282.0 %reduce-scatter.5.cloned.1.call-start = ((), (), s32[]{:S(2)}) async-start(), calls=%async_computation.5 | async-start | bytes 17825792 | tf_op jit(solution)/shard_map/reduce_scatter | solution.py:81
  143.4 5.8 %copy-start.5 = (f32[8192]{0:T(1024)S(1)}, f32[8192]{0:T(1024)}, u32[]{:S(2)}) copy-start(f32[8192]{0:T(1024)} %param.13) | copy-start | bytes 98308
  148.8 3.4 copy-start.4
  166.5 224.1 %reduce-scatter.7.cloned.1.call-start = ((), (), s32[]{:S(2)}) async-start(), calls=%async_computation.6 | async-start | bytes 1114112
Sparse Core Ops, SparseCore 0:
  34.4 78.0 all-gather.1
  166.7 149.6 reduce-scatter.4
  319.0 71.5 reduce-scatter.6
